TPU v7x, 512 devices: a whole 4x8x8 slice. The times are simulated.
512 devices in a mesh: ch: 128 (over y, z, core), grp: 4 (over x).
Axes of the slice: x: 4, y: 8, z: 8, core: 2. Of those that a mesh axis runs over, the one named last changes fastest.
Arguments:
- raw: bfloat16 [4, 1024, 2048], P('grp', 'ch'), may hold values from -400 to 400
- order: int32 [128, 16], P('ch'), may hold values from 0 to 15, each once within a row
- pair_blocks: int32 [128, 3], P('ch'), may hold values from -1 to 15, as said below
Outputs:
- corr: bfloat16 [2048, 3, 128, 256], P(('ch', 'grp'))
Inputs may be any that keep to these rules, and one draw needn't show every extreme that they name: `pair_blocks`: row i names distinct blocks among i * 16 // 128 - 1, i * 16 // 128, i * 16 // 128 + 1 that lie in 0 .. 15; slot 0 is always i * 16 // 128; live slots come first and empty ones hold -1.
All inputs are finite; a program needn't handle non-finite values.
Results may differ from a plain program's by a relative error of at most 0.013.
Values may be sent and summed in bfloat16 or wider, within the bound.
A program may use at most 128 MiB of HBM per device.

v0:
```python
import math

import jax
import jax.numpy as jnp
from jax import lax
from jax.sharding import PartitionSpec as P

SRC = 128
SEG = 256
LAGS = 256
SMOOTH = 8
MAXP = 3
REACH = 15


lag_scale = 1.0 / 16.0


def from_behind(value, axis, steps):
    count = lax.axis_size(axis)
    initial, last = (max(0, -steps), min(count, count - steps))
    return lax.ppermute(value, axis, [(source, source + steps) for source in range(initial, last)])


def transform_tables(half_len, lag_count, smooth_half):
    samples = jnp.arange(half_len, dtype=jnp.int32)
    column = jnp.arange(2 * half_len, dtype=jnp.int32)
    freq = column % half_len + 1
    phase_fwd = samples[:, None] * freq[None, :] % (2 * half_len)
    angle_fwd = phase_fwd.astype(jnp.float32) * (math.pi / half_len)
    forward = jnp.where(column[None, :] < half_len, jnp.cos(angle_fwd), -jnp.sin(angle_fwd)).astype(
        jnp.bfloat16
    )
    lag_steps = jnp.arange(lag_count, dtype=jnp.int32) - lag_count // 2
    phase_inv = freq[:, None] * lag_steps[None, :] % (2 * half_len)
    angle_inv = phase_inv.astype(jnp.float32) * (math.pi / half_len)
    inverse = (
        jnp.where(column[:, None] < half_len, jnp.cos(angle_inv), -jnp.sin(angle_inv)) * lag_scale
    ).astype(jnp.bfloat16)
    bins = jnp.arange(half_len, dtype=jnp.int32)
    smoothing = (jnp.abs(bins[:, None] - bins[None, :]) <= smooth_half).astype(jnp.float32) / (
        2 * smooth_half + 1
    )
    return (forward, inverse, smoothing)


def whiten(segments, forward, smoothing):
    half_len = segments.shape[-1]
    flat_rows = segments.reshape(-1, half_len)
    spectrum = jnp.dot(flat_rows, forward, preferred_element_type=jnp.float32)
    real_part = spectrum[:, :half_len]
    imag_part = spectrum[:, half_len:]
    power_bins = real_part * real_part + imag_part * imag_part
    smoothed = jnp.dot(power_bins, smoothing, precision=lax.Precision.HIGHEST)
    water_level = jnp.mean(power_bins, axis=1, keepdims=True)
    divisor = jnp.sqrt(smoothed + 0.1 * water_level + 1e-06)
    whitened = spectrum / jnp.concatenate([divisor, divisor], axis=1)
    return whitened.astype(jnp.bfloat16).reshape(segments.shape[:-1] + (2 * half_len,))


def correlate(receivers, sources, inverse):
    half_len = receivers.shape[-1] // 2
    seg_count = receivers.shape[1]
    recv_re = receivers[..., :half_len]
    recv_im = receivers[..., half_len:]
    left_first = jnp.concatenate([recv_re, recv_im], axis=1)
    left_second = jnp.concatenate([recv_im, -recv_re], axis=1)
    right_both = jnp.concatenate([sources[..., :half_len], sources[..., half_len:]], axis=1)
    cross_re = jnp.einsum(
        "rnk,snk->rsk", left_first, right_both, preferred_element_type=jnp.float32
    )
    cross_im = jnp.einsum(
        "rnk,snk->rsk", left_second, right_both, preferred_element_type=jnp.float32
    )
    cross_spec = (jnp.concatenate([cross_re, cross_im], axis=2) * (1.0 / seg_count)).astype(
        jnp.bfloat16
    )
    recv_count = receivers.shape[0]
    src_count = sources.shape[0]
    lag_values = jnp.dot(
        cross_spec.reshape(-1, 2 * half_len), inverse, preferred_element_type=jnp.float32
    )
    return lag_values.reshape(recv_count, src_count, inverse.shape[1])


def local(raw, order, pair_blocks):
    recorded = lax.all_to_all(raw, "ch", split_axis=2, concat_axis=1, tiled=True)
    local_channels = recorded.shape[2]
    onehot = (order[0][:, None] == jnp.arange(local_channels, dtype=jnp.int32)[None, :]).astype(
        jnp.bfloat16
    )
    series = jnp.einsum(
        "ck,tc->kt", onehot, recorded[0], preferred_element_type=jnp.float32
    ).astype(jnp.bfloat16)
    segments = series.reshape(1, local_channels, -1, SEG)
    forward, inverse, smoothing = transform_tables(SEG, LAGS, SMOOTH)
    own_white = whiten(segments, forward, smoothing)
    before_list = []
    for distance in range(REACH, 0, -1):
        before_list.append(from_behind(own_white, "ch", distance))
    after_list = []
    for distance in range(1, REACH + 1):
        after_list.append(from_behind(own_white, "ch", -distance))
    window = jnp.concatenate(before_list + [own_white] + after_list, axis=1)
    window_base = (lax.axis_index("ch") - REACH) * local_channels
    groups = lax.axis_size("grp")
    receivers = own_white[0]
    slot_results = []
    for slot_index in range(MAXP):
        block_id = pair_blocks[0, slot_index]
        source_start = jnp.maximum(block_id, 0) * SRC - window_base
        sources = lax.dynamic_slice_in_dim(window[0], source_start, SRC, 0)
        is_live = (block_id >= 0).astype(jnp.float32)
        lag_values = correlate(receivers, sources, inverse) * is_live
        slot_results.append(lag_values)
    stacked = lax.psum_scatter(
        jnp.stack(slot_results, axis=1).astype(jnp.bfloat16), "grp", scatter_dimension=0, tiled=True
    ).astype(jnp.float32)
    return (stacked / groups).astype(jnp.bfloat16)


def solution(mesh):
    placed = (P("grp", "ch", None), P("ch", None), P("ch", None))
    return jax.shard_map(
        local,
        mesh=mesh,
        in_specs=placed,
        out_specs=P(("ch", "grp"), None, None, None),
        check_vma=False,
    )
```

profile of v0, /device:TPU:1, one launch (start us, length us, event | category | flops | bytes accessed | tf_op | source)
XLA Modules:
  0.0 307.8 jit_solution(12834081129532482578)
XLA Ops:
  6.5 3.1 %copy.19 = bf16[1,8,2048]{1,0,2:T(2,128)(2,1)} copy(bf16[1,8,2048]{2,1,0:T(8,128)(2,1)} %param.3) | data formatting | bytes 65536 | tf_op args[0]
  9.7 18.5 %all-to-all-start = ((bf16[1,8,2048]{1,0,2:T(2,128)(2,1)}), bf16[1,8,2048]{1,0,2:T(2,128)(2,1)S(1)}, u32[]{:S(2)}, u32[]{:S(2)}) async-start(bf16[1,8,2048]{1,0,2:T(2,128)(2,1)} %copy.19), calls=%async_computation | async-start | bytes 2097152 | tf_op jit(solution)/shard_map/all_to_all | solution.py:87
  32.8 25.9 %all-to-all-done = bf16[1,8,2048]{1,0,2:T(2,128)(2,1)S(1)} async-done(((bf16[1,8,2048]{1,0,2:T(2,128)(2,1)}), bf16[1,8,2048]{1,0,2:T(2,128)(2,1)S(1)}, u32[]{:S(2)}, u32[]{:S(2)}) %all-to-all-start) | async-done | bytes 32800 | tf_op jit(solution)/shard_map/all_to_all | solution.py:87
  59.7 2.4 fusion.48
  62.6 4.5 %collective-permute-start = (bf16[1,16,4,512]{3,2,1,0:T(4,128)(2,1)S(1)}, bf16[1,16,4,512]{3,2,1,0:T(4,128)(2,1)S(1)}, u32[]{:S(2)}, u32[]{:S(2)}) collective-permute-start(bf16[1,16,4,512]{3,2,1,0:T(4,128)(2,1)S(1)} %reshape.97), channel_id=1, source_target_pairs={{0,60},{4,64},{8,68},{12,72},{16,76},{20,80},{24,84},{28,88},{32,9... | collective-permute-start | bytes 196616 | tf_op jit(solution)/shard_map/ppermute | solution.py:22
  68.4 3.3 %collective-permute-start.2 = (bf16[1,16,4,512]{3,2,1,0:T(4,128)(2,1)S(1)}, bf16[1,16,4,512]{3,2,1,0:T(4,128)(2,1)S(1)}, u32[]{:S(2)}, u32[]{:S(2)}) collective-permute-start(bf16[1,16,4,512]{3,2,1,0:T(4,128)(2,1)S(1)} %reshape.97), channel_id=1, source_target_pairs={{0,52},{4,56},{8,60},{12,64},{16,68},{20,72},{24,76},{28,80},{32,8... | collective-permute-start | bytes 196616 | tf_op jit(solution)/shard_map/ppermute | solution.py:22
  71.7 4.7 %collective-permute-start.3 = (bf16[1,16,4,512]{3,2,1,0:T(4,128)(2,1)S(1)}, bf16[1,16,4,512]{3,2,1,0:T(4,128)(2,1)S(1)}, u32[]{:S(2)}, u32[]{:S(2)}) collective-permute-start(bf16[1,16,4,512]{3,2,1,0:T(4,128)(2,1)S(1)} %reshape.97), channel_id=1, source_target_pairs={{0,48},{4,52},{8,56},{12,60},{16,64},{20,68},{24,72},{28,76},{32,8... | collective-permute-start | bytes 196616 | tf_op jit(solution)/shard_map/ppermute | solution.py:22
  76.5 4.3 %collective-permute-start.4 = (bf16[1,16,4,512]{3,2,1,0:T(4,128)(2,1)S(1)}, bf16[1,16,4,512]{3,2,1,0:T(4,128)(2,1)S(1)}, u32[]{:S(2)}, u32[]{:S(2)}) collective-permute-start(bf16[1,16,4,512]{3,2,1,0:T(4,128)(2,1)S(1)} %reshape.97), channel_id=1, source_target_pairs={{0,44},{4,48},{8,52},{12,56},{16,60},{20,64},{24,68},{28,72},{32,7... | collective-permute-start | bytes 196616 | tf_op jit(solution)/shard_map/ppermute | solution.py:22
  81.6 3.6 %collective-permute-start.5 = (bf16[1,16,4,512]{3,2,1,0:T(4,128)(2,1)S(1)}, bf16[1,16,4,512]{3,2,1,0:T(4,128)(2,1)S(1)}, u32[]{:S(2)}, u32[]{:S(2)}) collective-permute-start(bf16[1,16,4,512]{3,2,1,0:T(4,128)(2,1)S(1)} %reshape.97), channel_id=1, source_target_pairs={{0,40},{4,44},{8,48},{12,52},{16,56},{20,60},{24,64},{28,68},{32,7... | collective-permute-start | bytes 196616 | tf_op jit(solution)/shard_map/ppermute | solution.py:22
  85.3 5.7 %collective-permute-start.6 = (bf16[1,16,4,512]{3,2,1,0:T(4,128)(2,1)S(1)}, bf16[1,16,4,512]{3,2,1,0:T(4,128)(2,1)S(1)}, u32[]{:S(2)}, u32[]{:S(2)}) collective-permute-start(bf16[1,16,4,512]{3,2,1,0:T(4,128)(2,1)S(1)} %reshape.97), channel_id=1, source_target_pairs={{0,36},{4,40},{8,44},{12,48},{16,52},{20,56},{24,60},{28,64},{32,6... | collective-permute-start | bytes 196616 | tf_op jit(solution)/shard_map/ppermute | solution.py:22
  91.1 3.6 %collective-permute-start.7 = (bf16[1,16,4,512]{3,2,1,0:T(4,128)(2,1)S(1)}, bf16[1,16,4,512]{3,2,1,0:T(4,128)(2,1)S(1)}, u32[]{:S(2)}, u32[]{:S(2)}) collective-permute-start(bf16[1,16,4,512]{3,2,1,0:T(4,128)(2,1)S(1)} %reshape.97), channel_id=1, source_target_pairs={{0,32},{4,36},{8,40},{12,44},{16,48},{20,52},{24,56},{28,60},{32,6... | collective-permute-start | bytes 196616 | tf_op jit(solution)/shard_map/ppermute | solution.py:22
  94.8 7.2 %collective-permute-start.8 = (bf16[1,16,4,512]{3,2,1,0:T(4,128)(2,1)S(1)}, bf16[1,16,4,512]{3,2,1,0:T(4,128)(2,1)S(1)}, u32[]{:S(2)}, u32[]{:S(2)}) collective-permute-start(bf16[1,16,4,512]{3,2,1,0:T(4,128)(2,1)S(1)} %reshape.97), channel_id=1, source_target_pairs={{0,28},{4,32},{8,36},{12,40},{16,44},{20,48},{24,52},{28,56},{32,6... | collective-permute-start | bytes 196616 | tf_op jit(solution)/shard_map/ppermute | solution.py:22
  103.3 4.9 %collective-permute-start.10 = (bf16[1,16,4,512]{3,2,1,0:T(4,128)(2,1)S(1)}, bf16[1,16,4,512]{3,2,1,0:T(4,128)(2,1)S(1)}, u32[]{:S(2)}, u32[]{:S(2)}) collective-permute-start(bf16[1,16,4,512]{3,2,1,0:T(4,128)(2,1)S(1)} %reshape.97), channel_id=1, source_target_pairs={{0,20},{4,24},{8,28},{12,32},{16,36},{20,40},{24,44},{28,48},{32,5... | collective-permute-start | bytes 196616 | tf_op jit(solution)/shard_map/ppermute | solution.py:22
  108.3 4.0 %collective-permute-start.11 = (bf16[1,16,4,512]{3,2,1,0:T(4,128)(2,1)S(1)}, bf16[1,16,4,512]{3,2,1,0:T(4,128)(2,1)S(1)}, u32[]{:S(2)}, u32[]{:S(2)}) collective-permute-start(bf16[1,16,4,512]{3,2,1,0:T(4,128)(2,1)S(1)} %reshape.97), channel_id=1, source_target_pairs={{0,16},{4,20},{8,24},{12,28},{16,32},{20,36},{24,40},{28,44},{32,4... | collective-permute-start | bytes 196616 | tf_op jit(solution)/shard_map/ppermute | solution.py:22
  112.4 5.1 %collective-permute-start.12 = (bf16[1,16,4,512]{3,2,1,0:T(4,128)(2,1)S(1)}, bf16[1,16,4,512]{3,2,1,0:T(4,128)(2,1)S(1)}, u32[]{:S(2)}, u32[]{:S(2)}) collective-permute-start(bf16[1,16,4,512]{3,2,1,0:T(4,128)(2,1)S(1)} %reshape.97), channel_id=1, source_target_pairs={{0,12},{4,16},{8,20},{12,24},{16,28},{20,32},{24,36},{28,40},{32,4... | collective-permute-start | bytes 196616 | tf_op jit(solution)/shard_map/ppermute | solution.py:22
  119.3 2.7 collective-permute-start.14
  136.9 2.9 collective-permute-done.19
  141.1 2.4 collective-permute-done.20
  152.7 4.3 %collective-permute-done.25 = bf16[1,16,4,512]{3,2,1,0:T(4,128)(2,1)S(1)} collective-permute-done((bf16[1,16,4,512]{3,2,1,0:T(4,128)(2,1)S(1)}, bf16[1,16,4,512]{3,2,1,0:T(4,128)(2,1)S(1)}, u32[]{:S(2)}, u32[]{:S(2)}) %collective-permute-start.25) | collective-permute-done | bytes 65568 | tf_op jit(solution)/shard_map/ppermute | solution.py:22
  157.0 2.7 collective-permute-done.26
  159.7 8.3 %collective-permute-done.27 = bf16[1,16,4,512]{3,2,1,0:T(4,128)(2,1)S(1)} collective-permute-done((bf16[1,16,4,512]{3,2,1,0:T(4,128)(2,1)S(1)}, bf16[1,16,4,512]{3,2,1,0:T(4,128)(2,1)S(1)}, u32[]{:S(2)}, u32[]{:S(2)}) %collective-permute-start.27) | collective-permute-done | bytes 65568 | tf_op jit(solution)/shard_map/ppermute | solution.py:22
  168.6 2.2 collective-permute-done.29
  173.6 1.9 convolution_bitcast_fusion.4
  175.6 2.1 copy.26
  178.9 2.0 convolution_bitcast_fusion.3
  180.9 1.9 convolution_bitcast_fusion.2
  182.8 2.2 copy.30
  191.0 3.4 %fusion.15 = bf16[16,1,128,256]{3,2,0,1:T(8,128)(2,1)S(1)} fusion(bf16[16,128,512]{1,0,2:T(8,128)(2,1)S(1)} %fusion, f32[]{:T(128)} %bitcast.8, s32[256]{0:T(256)S(1)} %iota_add_fusion, s32[512]{0:T(512)S(1)} %fusion.63, pred[512]{0:T(512)(128)(4,1)S(1)} %iota_compare_fusion.1), kind=kOutput, calls=%fused_computation.23 | convolution fusion | flops 540278784 | bytes 3149316 | tf_op jit(solution)/shard_map/dot_general | solution.py:80
  194.4 3.4 %fusion.18 = bf16[16,1,128,256]{3,2,0,1:T(8,128)(2,1)S(1)} fusion(bf16[16,128,512]{1,0,2:T(8,128)(2,1)S(1)} %fusion.1, f32[]{:T(128)} %bitcast.14, s32[256]{0:T(256)S(1)} %iota_add_fusion, s32[512]{0:T(512)S(1)} %fusion.63, pred[512]{0:T(512)(128)(4,1)S(1)} %iota_compare_fusion.1), kind=kOutput, calls=%fused_computation.24 | convolution fusion | flops 540278784 | bytes 3149316 | tf_op jit(solution)/shard_map/dot_general | solution.py:80
  198.1 3.4 %fusion.21 = bf16[16,1,128,256]{3,2,0,1:T(8,128)(2,1)S(1)} fusion(bf16[16,128,512]{1,0,2:T(8,128)(2,1)S(1)} %fusion.2, f32[]{:T(128)} %bitcast.20, s32[256]{0:T(256)S(1)} %iota_add_fusion, s32[512]{0:T(512)S(1)} %fusion.63, pred[512]{0:T(512)(128)(4,1)S(1)} %iota_compare_fusion.1), kind=kOutput, calls=%fused_computation.25 | convolution fusion | flops 540278784 | bytes 3149316 | tf_op jit(solution)/shard_map/dot_general | solution.py:80
  201.5 2.0 pad_maximum_fusion
  205.5 93.2 %all-reduce.3.cloned.1.call-done = bf16[16,3,128,256]{3,2,0,1:T(8,128)(2,1)} async-done(((bf16[16,3,128,256]{3,2,0,1:T(8,128)(2,1)}), bf16[16,3,128,256]{3,2,0,1:T(8,128)(2,1)}) %all-reduce.3.cloned.1.call-update) | async-done | bytes 3145744
  (117 shorter events, 47.4 us)
Async XLA Ops:
  9.7 49.0 %all-to-all-start = ((bf16[1,8,2048]{1,0,2:T(2,128)(2,1)}), bf16[1,8,2048]{1,0,2:T(2,128)(2,1)S(1)}, u32[]{:S(2)}, u32[]{:S(2)}) async-start(bf16[1,8,2048]{1,0,2:T(2,128)(2,1)} %copy.19), calls=%async_computation | async-start | bytes 2097152 | tf_op jit(solution)/shard_map/all_to_all | solution.py:87
  28.2 270.5 %all-reduce.3.cloned.1.call-start = ((), (), s32[]{:S(2)}) async-start(), calls=%async_computation.1 | async-start | bytes 6291456
  62.6 19.0 %collective-permute-start = (bf16[1,16,4,512]{3,2,1,0:T(4,128)(2,1)S(1)}, bf16[1,16,4,512]{3,2,1,0:T(4,128)(2,1)S(1)}, u32[]{:S(2)}, u32[]{:S(2)}) collective-permute-start(bf16[1,16,4,512]{3,2,1,0:T(4,128)(2,1)S(1)} %reshape.97), channel_id=1, source_target_pairs={{0,60},{4,64},{8,68},{12,72},{16,76},{20,80},{24,84},{28,88},{32,9... | collective-permute-start | bytes 196616 | tf_op jit(solution)/shard_map/ppermute | solution.py:22
  67.1 18.2 %collective-permute-start.1 = (bf16[1,16,4,512]{3,2,1,0:T(4,128)(2,1)S(1)}, bf16[1,16,4,512]{3,2,1,0:T(4,128)(2,1)S(1)}, u32[]{:S(2)}, u32[]{:S(2)}) collective-permute-start(bf16[1,16,4,512]{3,2,1,0:T(4,128)(2,1)S(1)} %reshape.97), channel_id=1, source_target_pairs={{0,56},{4,60},{8,64},{12,68},{16,72},{20,76},{24,80},{28,84},{32,8... | collective-permute-start | bytes 196616 | tf_op jit(solution)/shard_map/ppermute | solution.py:22
  68.4 22.7 %collective-permute-start.2 = (bf16[1,16,4,512]{3,2,1,0:T(4,128)(2,1)S(1)}, bf16[1,16,4,512]{3,2,1,0:T(4,128)(2,1)S(1)}, u32[]{:S(2)}, u32[]{:S(2)}) collective-permute-start(bf16[1,16,4,512]{3,2,1,0:T(4,128)(2,1)S(1)} %reshape.97), channel_id=1, source_target_pairs={{0,52},{4,56},{8,60},{12,64},{16,68},{20,72},{24,76},{28,80},{32,8... | collective-permute-start | bytes 196616 | tf_op jit(solution)/shard_map/ppermute | solution.py:22
  71.7 23.0 %collective-permute-start.3 = (bf16[1,16,4,512]{3,2,1,0:T(4,128)(2,1)S(1)}, bf16[1,16,4,512]{3,2,1,0:T(4,128)(2,1)S(1)}, u32[]{:S(2)}, u32[]{:S(2)}) collective-permute-start(bf16[1,16,4,512]{3,2,1,0:T(4,128)(2,1)S(1)} %reshape.97), channel_id=1, source_target_pairs={{0,48},{4,52},{8,56},{12,60},{16,64},{20,68},{24,72},{28,76},{32,8... | collective-permute-start | bytes 196616 | tf_op jit(solution)/shard_map/ppermute | solution.py:22
  76.5 25.5 %collective-permute-start.4 = (bf16[1,16,4,512]{3,2,1,0:T(4,128)(2,1)S(1)}, bf16[1,16,4,512]{3,2,1,0:T(4,128)(2,1)S(1)}, u32[]{:S(2)}, u32[]{:S(2)}) collective-permute-start(bf16[1,16,4,512]{3,2,1,0:T(4,128)(2,1)S(1)} %reshape.97), channel_id=1, source_target_pairs={{0,44},{4,48},{8,52},{12,56},{16,60},{20,64},{24,68},{28,72},{32,7... | collective-permute-start | bytes 196616 | tf_op jit(solution)/shard_map/ppermute | solution.py:22
  81.6 21.7 %collective-permute-start.5 = (bf16[1,16,4,512]{3,2,1,0:T(4,128)(2,1)S(1)}, bf16[1,16,4,512]{3,2,1,0:T(4,128)(2,1)S(1)}, u32[]{:S(2)}, u32[]{:S(2)}) collective-permute-start(bf16[1,16,4,512]{3,2,1,0:T(4,128)(2,1)S(1)} %reshape.97), channel_id=1, source_target_pairs={{0,40},{4,44},{8,48},{12,52},{16,56},{20,60},{24,64},{28,68},{32,7... | collective-permute-start | bytes 196616 | tf_op jit(solution)/shard_map/ppermute | solution.py:22
  85.3 23.0 %collective-permute-start.6 = (bf16[1,16,4,512]{3,2,1,0:T(4,128)(2,1)S(1)}, bf16[1,16,4,512]{3,2,1,0:T(4,128)(2,1)S(1)}, u32[]{:S(2)}, u32[]{:S(2)}) collective-permute-start(bf16[1,16,4,512]{3,2,1,0:T(4,128)(2,1)S(1)} %reshape.97), channel_id=1, source_target_pairs={{0,36},{4,40},{8,44},{12,48},{16,52},{20,56},{24,60},{28,64},{32,6... | collective-permute-start | bytes 196616 | tf_op jit(solution)/shard_map/ppermute | solution.py:22
  91.1 21.3 %collective-permute-start.7 = (bf16[1,16,4,512]{3,2,1,0:T(4,128)(2,1)S(1)}, bf16[1,16,4,512]{3,2,1,0:T(4,128)(2,1)S(1)}, u32[]{:S(2)}, u32[]{:S(2)}) collective-permute-start(bf16[1,16,4,512]{3,2,1,0:T(4,128)(2,1)S(1)} %reshape.97), channel_id=1, source_target_pairs={{0,32},{4,36},{8,40},{12,44},{16,48},{20,52},{24,56},{28,60},{32,6... | collective-permute-start | bytes 196616 | tf_op jit(solution)/shard_map/ppermute | solution.py:22
  94.8 22.7 %collective-permute-start.8 = (bf16[1,16,4,512]{3,2,1,0:T(4,128)(2,1)S(1)}, bf16[1,16,4,512]{3,2,1,0:T(4,128)(2,1)S(1)}, u32[]{:S(2)}, u32[]{:S(2)}) collective-permute-start(bf16[1,16,4,512]{3,2,1,0:T(4,128)(2,1)S(1)} %reshape.97), channel_id=1, source_target_pairs={{0,28},{4,32},{8,36},{12,40},{16,44},{20,48},{24,52},{28,56},{32,6... | collective-permute-start | bytes 196616 | tf_op jit(solution)/shard_map/ppermute | solution.py:22
  102.0 17.3 %collective-permute-start.9 = (bf16[1,16,4,512]{3,2,1,0:T(4,128)(2,1)S(1)}, bf16[1,16,4,512]{3,2,1,0:T(4,128)(2,1)S(1)}, u32[]{:S(2)}, u32[]{:S(2)}) collective-permute-start(bf16[1,16,4,512]{3,2,1,0:T(4,128)(2,1)S(1)} %reshape.97), channel_id=1, source_target_pairs={{0,24},{4,28},{8,32},{12,36},{16,40},{20,44},{24,48},{28,52},{32,5... | collective-permute-start | bytes 196616 | tf_op jit(solution)/shard_map/ppermute | solution.py:22
  103.3 18.7 %collective-permute-start.10 = (bf16[1,16,4,512]{3,2,1,0:T(4,128)(2,1)S(1)}, bf16[1,16,4,512]{3,2,1,0:T(4,128)(2,1)S(1)}, u32[]{:S(2)}, u32[]{:S(2)}) collective-permute-start(bf16[1,16,4,512]{3,2,1,0:T(4,128)(2,1)S(1)} %reshape.97), channel_id=1, source_target_pairs={{0,20},{4,24},{8,28},{12,32},{16,36},{20,40},{24,44},{28,48},{32,5... | collective-permute-start | bytes 196616 | tf_op jit(solution)/shard_map/ppermute | solution.py:22
  108.3 15.6 %collective-permute-start.11 = (bf16[1,16,4,512]{3,2,1,0:T(4,128)(2,1)S(1)}, bf16[1,16,4,512]{3,2,1,0:T(4,128)(2,1)S(1)}, u32[]{:S(2)}, u32[]{:S(2)}) collective-permute-start(bf16[1,16,4,512]{3,2,1,0:T(4,128)(2,1)S(1)} %reshape.97), channel_id=1, source_target_pairs={{0,16},{4,20},{8,24},{12,28},{16,32},{20,36},{24,40},{28,44},{32,4... | collective-permute-start | bytes 196616 | tf_op jit(solution)/shard_map/ppermute | solution.py:22
  112.4 12.9 %collective-permute-start.12 = (bf16[1,16,4,512]{3,2,1,0:T(4,128)(2,1)S(1)}, bf16[1,16,4,512]{3,2,1,0:T(4,128)(2,1)S(1)}, u32[]{:S(2)}, u32[]{:S(2)}) collective-permute-start(bf16[1,16,4,512]{3,2,1,0:T(4,128)(2,1)S(1)} %reshape.97), channel_id=1, source_target_pairs={{0,12},{4,16},{8,20},{12,24},{16,28},{20,32},{24,36},{28,40},{32,4... | collective-permute-start | bytes 196616 | tf_op jit(solution)/shard_map/ppermute | solution.py:22
  117.5 9.2 %collective-permute-start.13 = (bf16[1,16,4,512]{3,2,1,0:T(4,128)(2,1)S(1)}, bf16[1,16,4,512]{3,2,1,0:T(4,128)(2,1)S(1)}, u32[]{:S(2)}, u32[]{:S(2)}) collective-permute-start(bf16[1,16,4,512]{3,2,1,0:T(4,128)(2,1)S(1)} %reshape.97), channel_id=1, source_target_pairs={{0,8},{4,12},{8,16},{12,20},{16,24},{20,28},{24,32},{28,36},{32,40... | collective-permute-start | bytes 196616 | tf_op jit(solution)/shard_map/ppermute | solution.py:22
  119.3 8.8 %collective-permute-start.14 = (bf16[1,16,4,512]{3,2,1,0:T(4,128)(2,1)S(1)}, bf16[1,16,4,512]{3,2,1,0:T(4,128)(2,1)S(1)}, u32[]{:S(2)}, u32[]{:S(2)}) collective-permute-start(bf16[1,16,4,512]{3,2,1,0:T(4,128)(2,1)S(1)} %reshape.97), channel_id=1, source_target_pairs={{0,4},{4,8},{8,12},{12,16},{16,20},{20,24},{24,28},{28,32},{32,36}... | collective-permute-start | bytes 196616 | tf_op jit(solution)/shard_map/ppermute | solution.py:22
  122.0 7.4 %collective-permute-start.15 = (bf16[1,16,4,512]{3,2,1,0:T(4,128)(2,1)S(1)}, bf16[1,16,4,512]{3,2,1,0:T(4,128)(2,1)S(1)}, u32[]{:S(2)}, u32[]{:S(2)}) collective-permute-start(bf16[1,16,4,512]{3,2,1,0:T(4,128)(2,1)S(1)} %reshape.97), channel_id=1, source_target_pairs={{4,0},{8,4},{12,8},{16,12},{20,16},{24,20},{28,24},{32,28},{36,32}... | collective-permute-start | bytes 196616 | tf_op jit(solution)/shard_map/ppermute | solution.py:22
  124.0 6.8 %collective-permute-start.16 = (bf16[1,16,4,512]{3,2,1,0:T(4,128)(2,1)S(1)}, bf16[1,16,4,512]{3,2,1,0:T(4,128)(2,1)S(1)}, u32[]{:S(2)}, u32[]{:S(2)}) collective-permute-start(bf16[1,16,4,512]{3,2,1,0:T(4,128)(2,1)S(1)} %reshape.97), channel_id=1, source_target_pairs={{8,0},{12,4},{16,8},{20,12},{24,16},{28,20},{32,24},{36,28},{40,32... | collective-permute-start | bytes 196616 | tf_op jit(solution)/shard_map/ppermute | solution.py:22
  125.3 8.3 %collective-permute-start.17 = (bf16[1,16,4,512]{3,2,1,0:T(4,128)(2,1)S(1)}, bf16[1,16,4,512]{3,2,1,0:T(4,128)(2,1)S(1)}, u32[]{:S(2)}, u32[]{:S(2)}) collective-permute-start(bf16[1,16,4,512]{3,2,1,0:T(4,128)(2,1)S(1)} %reshape.97), channel_id=1, source_target_pairs={{12,0},{16,4},{20,8},{24,12},{28,16},{32,20},{36,24},{40,28},{44,3... | collective-permute-start | bytes 196616 | tf_op jit(solution)/shard_map/ppermute | solution.py:22
  126.7 8.9 %collective-permute-start.18 = (bf16[1,16,4,512]{3,2,1,0:T(4,128)(2,1)S(1)}, bf16[1,16,4,512]{3,2,1,0:T(4,128)(2,1)S(1)}, u32[]{:S(2)}, u32[]{:S(2)}) collective-permute-start(bf16[1,16,4,512]{3,2,1,0:T(4,128)(2,1)S(1)} %reshape.97), channel_id=1, source_target_pairs={{16,0},{20,4},{24,8},{28,12},{32,16},{36,20},{40,24},{44,28},{48,3... | collective-permute-start | bytes 196616 | tf_op jit(solution)/shard_map/ppermute | solution.py:22
  128.0 11.7 %collective-permute-start.19 = (bf16[1,16,4,512]{3,2,1,0:T(4,128)(2,1)S(1)}, bf16[1,16,4,512]{3,2,1,0:T(4,128)(2,1)S(1)}, u32[]{:S(2)}, u32[]{:S(2)}) collective-permute-start(bf16[1,16,4,512]{3,2,1,0:T(4,128)(2,1)S(1)} %reshape.97), channel_id=1, source_target_pairs={{20,0},{24,4},{28,8},{32,12},{36,16},{40,20},{44,24},{48,28},{52,3... | collective-permute-start | bytes 196616 | tf_op jit(solution)/shard_map/ppermute | solution.py:22
  129.4 14.1 %collective-permute-start.20 = (bf16[1,16,4,512]{3,2,1,0:T(4,128)(2,1)S(1)}, bf16[1,16,4,512]{3,2,1,0:T(4,128)(2,1)S(1)}, u32[]{:S(2)}, u32[]{:S(2)}) collective-permute-start(bf16[1,16,4,512]{3,2,1,0:T(4,128)(2,1)S(1)} %reshape.97), channel_id=1, source_target_pairs={{24,0},{28,4},{32,8},{36,12},{40,16},{44,20},{48,24},{52,28},{56,3... | collective-permute-start | bytes 196616 | tf_op jit(solution)/shard_map/ppermute | solution.py:22
  130.8 14.1 %collective-permute-start.21 = (bf16[1,16,4,512]{3,2,1,0:T(4,128)(2,1)S(1)}, bf16[1,16,4,512]{3,2,1,0:T(4,128)(2,1)S(1)}, u32[]{:S(2)}, u32[]{:S(2)}) collective-permute-start(bf16[1,16,4,512]{3,2,1,0:T(4,128)(2,1)S(1)} %reshape.97), channel_id=1, source_target_pairs={{28,0},{32,4},{36,8},{40,12},{44,16},{48,20},{52,24},{56,28},{60,3... | collective-permute-start | bytes 196616 | tf_op jit(solution)/shard_map/ppermute | solution.py:22
  133.6 12.7 %collective-permute-start.22 = (bf16[1,16,4,512]{3,2,1,0:T(4,128)(2,1)S(1)}, bf16[1,16,4,512]{3,2,1,0:T(4,128)(2,1)S(1)}, u32[]{:S(2)}, u32[]{:S(2)}) collective-permute-start(bf16[1,16,4,512]{3,2,1,0:T(4,128)(2,1)S(1)} %reshape.97), channel_id=1, source_target_pairs={{32,0},{36,4},{40,8},{44,12},{48,16},{52,20},{56,24},{60,28},{64,3... | collective-permute-start | bytes 196616 | tf_op jit(solution)/shard_map/ppermute | solution.py:22
  135.6 13.1 %collective-permute-start.23 = (bf16[1,16,4,512]{3,2,1,0:T(4,128)(2,1)S(1)}, bf16[1,16,4,512]{3,2,1,0:T(4,128)(2,1)S(1)}, u32[]{:S(2)}, u32[]{:S(2)}) collective-permute-start(bf16[1,16,4,512]{3,2,1,0:T(4,128)(2,1)S(1)} %reshape.97), channel_id=1, source_target_pairs={{36,0},{40,4},{44,8},{48,12},{52,16},{56,20},{60,24},{64,28},{68,3... | collective-permute-start | bytes 196616 | tf_op jit(solution)/shard_map/ppermute | solution.py:22
  139.8 11.6 %collective-permute-start.24 = (bf16[1,16,4,512]{3,2,1,0:T(4,128)(2,1)S(1)}, bf16[1,16,4,512]{3,2,1,0:T(4,128)(2,1)S(1)}, u32[]{:S(2)}, u32[]{:S(2)}) collective-permute-start(bf16[1,16,4,512]{3,2,1,0:T(4,128)(2,1)S(1)} %reshape.97), channel_id=1, source_target_pairs={{40,0},{44,4},{48,8},{52,12},{56,16},{60,20},{64,24},{68,28},{72,3... | collective-permute-start | bytes 196616 | tf_op jit(solution)/shard_map/ppermute | solution.py:22
  143.5 13.5 %collective-permute-start.25 = (bf16[1,16,4,512]{3,2,1,0:T(4,128)(2,1)S(1)}, bf16[1,16,4,512]{3,2,1,0:T(4,128)(2,1)S(1)}, u32[]{:S(2)}, u32[]{:S(2)}) collective-permute-start(bf16[1,16,4,512]{3,2,1,0:T(4,128)(2,1)S(1)} %reshape.97), channel_id=1, source_target_pairs={{44,0},{48,4},{52,8},{56,12},{60,16},{64,20},{68,24},{72,28},{76,3... | collective-permute-start | bytes 196616 | tf_op jit(solution)/shard_map/ppermute | solution.py:22
  144.8 14.9 %collective-permute-start.26 = (bf16[1,16,4,512]{3,2,1,0:T(4,128)(2,1)S(1)}, bf16[1,16,4,512]{3,2,1,0:T(4,128)(2,1)S(1)}, u32[]{:S(2)}, u32[]{:S(2)}) collective-permute-start(bf16[1,16,4,512]{3,2,1,0:T(4,128)(2,1)S(1)} %reshape.97), channel_id=1, source_target_pairs={{48,0},{52,4},{56,8},{60,12},{64,16},{68,20},{72,24},{76,28},{80,3... | collective-permute-start | bytes 196616 | tf_op jit(solution)/shard_map/ppermute | solution.py:22
  146.3 21.7 %collective-permute-start.27 = (bf16[1,16,4,512]{3,2,1,0:T(4,128)(2,1)S(1)}, bf16[1,16,4,512]{3,2,1,0:T(4,128)(2,1)S(1)}, u32[]{:S(2)}, u32[]{:S(2)}) collective-permute-start(bf16[1,16,4,512]{3,2,1,0:T(4,128)(2,1)S(1)} %reshape.97), channel_id=1, source_target_pairs={{52,0},{56,4},{60,8},{64,12},{68,16},{72,20},{76,24},{80,28},{84,3... | collective-permute-start | bytes 196616 | tf_op jit(solution)/shard_map/ppermute | solution.py:22
  148.7 19.8 %collective-permute-start.28 = (bf16[1,16,4,512]{3,2,1,0:T(4,128)(2,1)S(1)}, bf16[1,16,4,512]{3,2,1,0:T(4,128)(2,1)S(1)}, u32[]{:S(2)}, u32[]{:S(2)}) collective-permute-start(bf16[1,16,4,512]{3,2,1,0:T(4,128)(2,1)S(1)} %reshape.97), channel_id=1, source_target_pairs={{56,0},{60,4},{64,8},{68,12},{72,16},{76,20},{80,24},{84,28},{88,3... | collective-permute-start | bytes 196616 | tf_op jit(solution)/shard_map/ppermute | solution.py:22
  151.4 19.3 %collective-permute-start.29 = (bf16[1,16,4,512]{3,2,1,0:T(4,128)(2,1)S(1)}, bf16[1,16,4,512]{3,2,1,0:T(4,128)(2,1)S(1)}, u32[]{:S(2)}, u32[]{:S(2)}) collective-permute-start(bf16[1,16,4,512]{3,2,1,0:T(4,128)(2,1)S(1)} %reshape.97), channel_id=1, source_target_pairs={{60,0},{64,4},{68,8},{72,12},{76,16},{80,20},{84,24},{88,28},{92,3... | collective-permute-start | bytes 196616 | tf_op jit(solution)/shard_map/ppermute | solution.py:22
  (5 other events, 76.9 us)
Sparse Core Ops, SparseCore 0:
  203.7 94.9 all-reduce.2
where the time goes:
time: 309 us; the launch traced here: 308 us
  waiting for transfers between devices  147 us (48%)
  starting transfers between devices  96.5 us (31%)
  matrix products  20.7 us (7%)
  local copies, waits for them, and re-layouts  20.3 us (7%)
  between operations  18.6 us (6%)
  other arithmetic  4.67 us (2%)
    unnamed x2, waiting for transfers between devices  93.2 us
    ppermute x30, starting transfers between devices, from_behind(): lax.ppermute(value, axis, [(source, source + steps) for source in range(i...  77.9 us
    ppermute x30, waiting for transfers between devices, from_behind(): lax.ppermute(value, axis, [(source, source + steps) for source in range(i...  27.9 us
    all_to_all x1, waiting for transfers between devices, local(): lax.all_to_all(raw, 'ch', split_axis=2, concat_axis=1, tiled=True)  25.9 us
    all_to_all x1, starting transfers between devices, local(): lax.all_to_all(raw, 'ch', split_axis=2, concat_axis=1, tiled=True)  18.5 us
    dot_general x3, matrix products, correlate(): jnp.dot(cross_spec.reshape(-1, 2 * half_len), inverse, preferred_element_...  10.2 us
    unnamed x42, local copies, waits for them, and re-layouts  8.24 us
    dynamic_slice x4, local copies, waits for them, and re-layouts, local(): sources = lax.dynamic_slice_in_dim(window[0], source_start, SRC, 0)  6.39 us
  transfers between devices with their start and end apart: 32, of which 14 were waited for; matrix products, arithmetic and copies ran while one was open for 1% of the time, Pallas kernels for 0%

commit v1 on v0

v1 whole, which is shorter than its diff:
```python
import math

import jax
import jax.numpy as jnp
import numpy as np
from jax import lax
from jax.experimental import pallas as pl
from jax.experimental.pallas import tpu as pltpu
from jax.sharding import PartitionSpec as P

CH_DEV = 16
SRC = 128
SEG = 256
LAGS = 256
SMOOTH = 8
MAXP = 3
NSEG = 4
WINDOWS = 4
ROWS = 8
Y, Z, C = 8, 8, 2
RECV = 4
WIDE = 512
SPAN = 384
BINS = 16
NWS = WINDOWS * NSEG
BF16 = jnp.bfloat16
F32 = jnp.float32
MESH = pl.DeviceIdType.MESH


def tables():
    place = np.arange(SEG)
    zc, parity, row = place // 16, place // 8 % 2, place % 8
    sample = parity * 128 + zc * 8 + row
    column = np.arange(2 * SEG)
    freq = column % SEG + 1
    angle = (sample[None, :] * freq[:, None] % (2 * SEG)) * (math.pi / SEG)
    real = column[:, None] < SEG
    forward = np.where(real, np.cos(angle), -np.sin(angle))
    lag = np.arange(LAGS) - LAGS // 2
    angle = (freq[None, :] * lag[:, None] % (2 * SEG)) * (math.pi / SEG)
    inverse = np.where(real.T, np.cos(angle), -np.sin(angle)) / 16.0
    return jnp.asarray(forward, BF16), jnp.asarray(inverse, BF16)


def start_block(y):
    return jnp.clip(2 * y - 1, 0, 12)


def first_lane_block(y, half):
    return jnp.where(y == 0, 0, jnp.where(y == Y - 1, 1, half))


def gather_kernel(raw, order, buf, ords, tile, y_send, y_recv, o_send, o_recv, q_send, q_recv, z_send, z_recv, p_send, p_recv, x_send, x_recv, own_sem):
    i = lax.axis_index("ch")
    x = lax.axis_index("grp")
    y, z, c = i // 16, i // 2 % Z, i % 2
    half = z // 4

    def ch(yy, zz, cc):
        return (yy * Z + zz) * C + cc

    def peer(yy, zz, cc, xx):
        return {"ch": ch(yy, zz, cc), "grp": xx}

    barrier = pltpu.get_barrier_semaphore()
    peers = [peer((y + d) % Y, z, c, x) for d in range(1, Y)]
    row = []
    for d in range(Z):
        for e in range(C):
            if d or e:
                row.append((d, e))
    peers += [peer(y, (z + d) % Z, (c + e) % C, x) for d, e in row]
    peers += [peer(y, z, c, (x + 1) % WINDOWS), peer(y, z, c, (x + 3) % WINDOWS)]
    for device in peers:
        pl.semaphore_signal(barrier, inc=1, device_id=device, device_id_type=MESH)

    base = i % 8 * CH_DEV
    lanes = lax.broadcasted_iota(jnp.int32, (16, 128), 1)
    placed = jnp.zeros((16, 128), jnp.int32)
    for j in range(CH_DEV):
        placed = jnp.where(lanes == base + j, base + order[0, j], placed)
    tile[0] = placed.astype(F32).astype(BF16)

    pl.semaphore_wait(barrier, len(peers))

    sends = []

    def send(src, dst, s_sem, r_sem, device):
        copy = pltpu.make_async_remote_copy(
            src_ref=src, dst_ref=dst, send_sem=s_sem, recv_sem=r_sem, device_id=device, device_id_type=MESH
        )
        copy.start()
        sends.append(copy)
        return copy

    seg, parity = y // 2, y % 2

    def landing():
        return buf.at[x, z, c, seg, pl.ds(pl.multiple_of(parity * ROWS, ROWS), ROWS), :]

    def wanted(yy):
        return raw.at[0, :, pl.ds(pl.multiple_of(start_block(yy) * SRC, SRC), WIDE)]

    waits = []
    for d in range(1, Y):
        yy = (y + d) % Y
        waits.append(send(wanted(yy), landing(), y_send.at[d - 1], y_recv.at[d - 1], peer(yy, z, c, x)))
    toward = (y + jnp.where(half == 1, 1, Y - 1)) % Y
    order_copy = send(tile.at[0], tile.at[1], o_send.at[0], o_recv.at[0], peer(toward, z, c, x))
    own = pltpu.make_async_copy(wanted(y), landing(), own_sem)
    own.start()

    order_copy.wait_recv()
    order_waits = []
    for n, (d, e) in enumerate(row):
        order_waits.append(
            send(tile, ords.at[z, c], q_send.at[n], q_recv.at[n], peer(y, (z + d) % Z, (c + e) % C, x))
        )
    own_order = pltpu.make_async_copy(tile, ords.at[z, c], o_send.at[1])
    own_order.start()

    for copy in waits:
        copy.wait_recv()
    own.wait()

    lane = pl.ds(pl.multiple_of(first_lane_block(y, half) * SRC, SRC), SPAN)

    def part(w, zz, cc, first=0, count=NSEG):
        return buf.at[w, zz, cc, pl.ds(first, count), :, lane]

    received = {}

    def to_partner(w_rel, d):
        w, zz = (x + w_rel) % WINDOWS, (z + d) % Z
        n = w_rel * Z + d
        copy = send(part(w, zz, c), part(w, zz, c), p_send.at[n], p_recv.at[n], peer(y, z, (c + 1) % C, x))
        received["p", n] = copy

    def to_x(d):
        zz = (z + d) % Z
        for side, step in ((0, 1), (1, WINDOWS - 1)):
            copy = send(
                part(x, zz, c), part(x, zz, c), x_send.at[side, d], x_recv.at[side, d], peer(y, z, c, (x + step) % WINDOWS)
            )
            received["x", side, d] = copy

    def forward_x(d):
        zz = (z + d) % Z
        for side, w_rel, step, first in ((0, WINDOWS - 1, 1, 0), (1, 1, WINDOWS - 1, 2)):
            received["x", side, d].wait_recv()
            w = (x + w_rel) % WINDOWS
            copy = send(
                part(w, zz, c, first, 2),
                part(w, zz, c, first, 2),
                x_send.at[2 + side, d],
                x_recv.at[2 + side, d],
                peer(y, z, c, (x + step) % WINDOWS),
            )
            received["x", 2 + side, d] = copy
            to_partner(w_rel, d)

    def along_z(side, hop, zz, first, count):
        step = 1 if side == 0 else Z - 1
        ref = buf.at[x, zz, c, pl.ds(first, count)]
        copy = send(ref, ref, z_send.at[side, hop - 1], z_recv.at[side, hop - 1], peer(y, (z + step) % Z, c, x))
        received["z", side, hop] = copy

    along_z(0, 1, z, 0, NSEG)
    along_z(1, 1, z, 0, NSEG)
    to_x(0)
    to_partner(0, 0)
    for hop in range(1, 4):
        for side, d in ((0, Z - hop), (1, hop)):
            received["z", side, hop].wait_recv()
            zz = (z + d) % Z
            if hop < 3:
                along_z(side, hop + 1, zz, 0, NSEG)
            else:
                along_z(side, hop + 1, zz, 2 * side, 2)
            to_x(d)
            to_partner(0, d)
    received["z", 0, 4].wait_recv()
    received["z", 1, 4].wait_recv()
    to_x(4)
    to_partner(0, 4)

    arrival = [0, 7, 1, 6, 2, 5, 3, 4]
    for d in arrival:
        forward_x(d)
    for d in arrival:
        received["x", 2, d].wait_recv()
        received["x", 3, d].wait_recv()
        to_partner(2, d)
    for w_rel in (0, 1, 3, 2):
        for d in range(Z):
            received["p", w_rel * Z + d].wait_recv()
    for copy in order_waits:
        copy.wait_recv()
    own_order.wait()
    for copy in sends:
        copy.wait_send()


def gather(raw, order):
    dma = pltpu.SemaphoreType.DMA
    return pl.pallas_call(
        gather_kernel,
        out_shape=(
            jax.ShapeDtypeStruct((WINDOWS, Z, C, NSEG, 16, WIDE), BF16),
            jax.ShapeDtypeStruct((Z, C, 2, 16, 128), BF16),
        ),
        in_specs=[pl.BlockSpec(memory_space=pltpu.VMEM), pl.BlockSpec(memory_space=pltpu.SMEM)],
        out_specs=[pl.BlockSpec(memory_space=pltpu.VMEM)] * 2,
        scratch_shapes=[
            pltpu.VMEM((2, 16, 128), BF16),
            dma((Y - 1,)),
            dma((Y - 1,)),
            dma((2,)),
            dma((1,)),
            dma((15,)),
            dma((15,)),
            dma((2, 4)),
            dma((2, 4)),
            dma((WINDOWS * Z,)),
            dma((WINDOWS * Z,)),
            dma((4, Z)),
            dma((4, Z)),
            dma,
        ],
        compiler_params=pltpu.CompilerParams(collective_id=0, has_side_effects=True, vmem_limit_bytes=32 << 20),
        name="gather",
    )(raw, order)


def dot(a, b, dims=((1,), (0,))):
    return lax.dot_general(a, b, (dims, ((), ())), preferred_element_type=F32)


NT = ((1,), (1,))


def correlate_kernel(pairs, place, buf, ords, forward, inverse, out, white, pos, left, cross, lagged):
    y, half, block, g, first = place[0], place[1], place[2], place[3], place[4]
    start = start_block(y) + first
    lane = pl.multiple_of(first * SRC, SRC)

    for n, (upper, which) in enumerate(((1, 1), (0, 0), (1, 0), (0, 1))):
        total = jnp.zeros((16, 128), F32)
        for zz in range(4):
            for cc in range(C):
                total = total + ords[upper * 4 + zz, cc, which].astype(F32)
        pos[n] = total

    def iota(shape, axis):
        return lax.broadcasted_iota(jnp.int32, shape, axis)

    band = (jnp.abs(iota((SEG, SEG), 0) - iota((SEG, SEG), 1)) <= SMOOTH).astype(F32).astype(BF16)

    def whiten(ws, carry):
        w, seg = ws // NSEG, ws % NSEG
        samples = buf[w, :, :, seg, :, pl.ds(lane, SPAN)].reshape(SEG, SPAN)
        spectrum = dot(forward[...], samples)
        real, imag = spectrum[:SEG], spectrum[SEG:]
        power = real * real + imag * imag
        level = jnp.sum(power, axis=0, keepdims=True) * (0.1 / SEG)
        smoothed = dot(band, power.astype(BF16)) * (1.0 / (2 * SMOOTH + 1))
        scale = lax.rsqrt(smoothed + level + 1e-6)
        white[ws, :SEG] = (real * scale).astype(BF16)
        white[ws, SEG:] = (imag * scale).astype(BF16)
        return carry

    lax.fori_loop(0, NWS, whiten, 0)

    mine = pos[1 + half][:1].astype(jnp.int32)
    rows = iota((128, 128), 0)
    target = block % 8 * CH_DEV + g * RECV + rows // 16
    hit = (mine == target) & (rows < RECV * NWS)
    own_lane = pl.multiple_of((block // 8 - start) * SRC, SRC)

    def pick(ws, total):
        choice = (hit & (rows % 16 == ws)).astype(F32).astype(BF16)
        return total + dot(white[ws, :, pl.ds(own_lane, SRC)], choice, NT)

    picked = lax.fori_loop(0, NWS, pick, jnp.zeros((2 * SEG, 128), F32)).astype(BF16)
    expand = (iota((128, RECV * 256), 0) == iota((128, RECV * 256), 1) // 16).astype(F32).astype(BF16)
    keep = iota((2 * SEG, RECV * 256), 0) % BINS == iota((2 * SEG, RECV * 256), 1) % BINS
    left[...] = jnp.where(keep, dot(picked, expand), 0.0).astype(BF16)

    def bins(q, carry):
        at = pl.multiple_of(q * BINS, BINS)
        re = left[pl.ds(at, BINS), :]
        im = left[pl.ds(SEG + at, BINS), :]
        lhs = []
        for r in range(RECV):
            one = slice(r * 256, r * 256 + 256)
            lhs.append(jnp.concatenate([re[:, one], im[:, one]], axis=1))
            lhs.append(jnp.concatenate([im[:, one], -re[:, one]], axis=1))
        lhs = jnp.concatenate(lhs, axis=0)
        right_re = white[:, pl.ds(at, BINS), :].reshape(256, SPAN)
        right_im = white[:, pl.ds(SEG + at, BINS), :].reshape(256, SPAN)
        right = jnp.concatenate([right_re, right_im], axis=0)
        product = (dot(lhs, right) * (1.0 / (NSEG * WINDOWS))).astype(BF16)
        for r in range(RECV):
            cross[r, pl.ds(at, BINS), :] = product[r * 2 * BINS : r * 2 * BINS + BINS]
            cross[r, pl.ds(SEG + at, BINS), :] = product[r * 2 * BINS + BINS : (r + 1) * 2 * BINS]
        return carry

    lax.fori_loop(0, SEG // BINS, bins, 0)

    for r in range(RECV):
        value = dot(inverse[...], cross[r]).astype(BF16)
        for n in range(SPAN // SRC):
            lagged[n, r] = value[:, n * SRC : n * SRC + SRC]

    for p in range(MAXP):
        b = pairs[0, p]
        live = b >= 0
        source = jnp.where(live, b - start, 0)
        where_to = pos[jnp.where(live, b - (2 * y - 1), 1)][:1].astype(jnp.int32)
        turn = ((iota((SRC, SRC), 0) == where_to) & live).astype(F32).astype(BF16)
        for r in range(RECV):
            out[r, p] = dot(turn, lagged[source, r], NT).astype(BF16)


def correlate(pairs, place, buf, ords, forward, inverse):
    smem = pl.BlockSpec(memory_space=pltpu.SMEM)
    vmem = pl.BlockSpec(memory_space=pltpu.VMEM)
    return pl.pallas_call(
        correlate_kernel,
        out_shape=jax.ShapeDtypeStruct((RECV, MAXP, SRC, LAGS), BF16),
        in_specs=[smem, smem, vmem, vmem, vmem, vmem],
        out_specs=vmem,
        scratch_shapes=[
            pltpu.VMEM((NWS, 2 * SEG, SPAN), BF16),
            pltpu.VMEM((4, 16, 128), F32),
            pltpu.VMEM((2 * SEG, RECV * 256), BF16),
            pltpu.VMEM((RECV, 2 * SEG, SPAN), BF16),
            pltpu.VMEM((SPAN // SRC, RECV, LAGS, SRC), BF16),
        ],
        compiler_params=pltpu.CompilerParams(vmem_limit_bytes=48 << 20),
        name="correlate",
    )(pairs, place, buf, ords, forward, inverse)


def local(raw, order, pair_blocks):
    buf, ords = gather(raw, order)
    forward, inverse = tables()
    i, g = lax.axis_index("ch"), lax.axis_index("grp")
    y, half = i // 16, i // 8 % 2
    place = jnp.stack([y, half, i, g, first_lane_block(y, half)]).astype(jnp.int32)
    return correlate(pair_blocks, place, buf, ords, forward, inverse)


def solution(mesh):
    placed = (P("grp", "ch", None), P("ch", None), P("ch", None))
    return jax.shard_map(
        local,
        mesh=mesh,
        in_specs=placed,
        out_specs=P(("ch", "grp"), None, None, None),
        check_vma=False,
    )
```

time: 309 us -> 66.8 us (0.22)
  waiting for transfers between devices: 147 us -> 0 us
  starting transfers between devices: 96.5 us -> 0 us
  Pallas kernels: 0 us -> 62.5 us
  matrix products: 20.7 us -> 0 us
  between operations: 18.6 us -> 0.02 us
  local copies, waits for them, and re-layouts: 20.3 us -> 4.05 us
  other arithmetic: 4.67 us -> 0 us
    unnamed x2 -> x0, waiting for transfers between devices: 93.2 us -> none
    ppermute x30 -> x0, starting transfers between devices: 77.9 us -> none  [from_behind(): lax.ppermute(value, axis, [(source, source + steps) for source in range(i...]
    pallas_call x0 -> x2, Pallas kernels: none -> 62.5 us  [the longest x1 43.9 us: gather(): pl.pallas_call(gather_kernel, out_shape=(jax.ShapeDtypeStruct((WINDOWS, Z...]
    ppermute x30 -> x0, waiting for transfers between devices: 27.9 us -> none  [from_behind(): lax.ppermute(value, axis, [(source, source + steps) for source in range(i...]
    all_to_all x1 -> x0, waiting for transfers between devices: 25.9 us -> none  [local(): lax.all_to_all(raw, 'ch', split_axis=2, concat_axis=1, tiled=True)]
    dot_general x12 -> x0, matrix products: 20.7 us -> none  [the longest x3 10.2 us: correlate(): jnp.dot(cross_spec.reshape(-1, 2 * half_len), inverse, preferred_element_...]
    all_to_all x1 -> x0, starting transfers between devices: 18.5 us -> none  [local(): lax.all_to_all(raw, 'ch', split_axis=2, concat_axis=1, tiled=True)]
    dynamic_slice x4 -> x0, local copies, waits for them, and re-layouts: 6.39 us -> none  [local(): sources = lax.dynamic_slice_in_dim(window[0], source_start, SRC, 0)]
  transfers between devices with their start and end apart: 32 -> 0, of which waited for: 14 -> 0; matrix products, arithmetic and copies ran while one was open for 1% -> 0% of each run, Pallas kernels for 0% -> 0%
where the time goes in v1:
time: 66.8 us; the launch traced here: 66.6 us
  Pallas kernels  62.5 us (94%)
  local copies, waits for them, and re-layouts  4.05 us (6%)
    pallas_call x1, Pallas kernels, gather(): pl.pallas_call(gather_kernel, out_shape=(jax.ShapeDtypeStruct((WINDOWS, Z...  43.9 us
    pallas_call x1, Pallas kernels, correlate(): pl.pallas_call(correlate_kernel, out_shape=jax.ShapeDtypeStruct((RECV, MA...  18.6 us
    unnamed x10, local copies, waits for them, and re-layouts  3.96 us

profile of v1, /device:TPU:1, one launch (start us, length us, event | category | flops | bytes accessed | tf_op | source)
XLA Modules:
  0.0 66.6 jit_solution(6148187739262133336)
XLA Ops:
  0.0 0.1 stack.23.place
  0.1 0.0 copy-start.2
  0.1 0.8 %copy-done.2 = bf16[1,8,2048]{2,1,0:T(8,128)(2,1)S(1)} copy-done((bf16[1,8,2048]{2,1,0:T(8,128)(2,1)S(1)}, bf16[1,8,2048]{2,1,0:T(8,128)(2,1)}, u32[]{:S(2)}) %copy-start.2) | copy-done | bytes 32792
  0.8 0.0 copy-start.3
  0.8 0.7 copy-done.3
  1.5 43.9 %gather.1 = (bf16[4,8,2,4,16,512]{5,4,3,2,1,0:T(8,128)(2,1)S(1)}, bf16[8,2,2,16,128]{4,3,2,1,0:T(8,128)(2,1)S(1)}) custom-call(bf16[1,8,2048]{2,1,0:T(8,128)(2,1)S(1)} %copy-done.2, s32[1,16]{1,0:T(1,128)S(1)} %copy-done.3), custom_call_target="tpu_custom_call" | custom-call | tf_op jit(solution)/shard_map/gather/pallas_call | solution.py:207
  45.4 0.0 copy-start
  45.5 0.9 %copy-done = bf16[256,512]{1,0:T(8,128)(2,1)S(1)} copy-done((bf16[256,512]{1,0:T(8,128)(2,1)S(1)}, bf16[256,512]{1,0:T(8,128)(2,1)}, u32[]{:S(2)}) %copy-start) | copy-done | bytes 262168
  46.4 0.0 copy-start.1
  46.4 0.9 %copy-done.1 = bf16[512,256]{1,0:T(8,128)(2,1)S(1)} copy-done((bf16[512,256]{1,0:T(8,128)(2,1)S(1)}, bf16[512,256]{1,0:T(8,128)(2,1)}, u32[]{:S(2)}) %copy-start.1) | copy-done | bytes 262168
  47.4 0.0 copy-start.4
  47.4 0.7 copy-done.4
  48.0 18.6 %correlate.1 = bf16[4,3,128,256]{3,2,1,0:T(8,128)(2,1)} custom-call(s32[1,3]{1,0:T(1,128)S(1)} %copy-done.4, s32[5]{0:T(128)S(1)} %stack.23.place, bf16[4,8,2,4,16,512]{5,4,3,2,1,0:T(8,128)(2,1)S(1)} %get-tuple-element.7.buf, bf16[8,2,2,16,128]{4,3,2,1,0:T(8,128)(2,1)S(1)} %get-tuple-element.8.ords, bf16[512,256]{1,0:T(8,128)(2,1)S(1)} %copy-done.1, ...), custom_call_target="tpu_custom_call" | custom-call | tf_op jit(solution)/shard_map/correlate/pallas_call | solution.py:329
Async XLA Ops:
  0.1 0.8 %copy-start.2 = (bf16[1,8,2048]{2,1,0:T(8,128)(2,1)S(1)}, bf16[1,8,2048]{2,1,0:T(8,128)(2,1)}, u32[]{:S(2)}) copy-start(bf16[1,8,2048]{2,1,0:T(8,128)(2,1)} %raw.1) | copy-start | bytes 98308
  0.8 0.7 copy-start.3
  45.4 1.0 %copy-start = (bf16[256,512]{1,0:T(8,128)(2,1)S(1)}, bf16[256,512]{1,0:T(8,128)(2,1)}, u32[]{:S(2)}) copy-start(bf16[256,512]{1,0:T(8,128)(2,1)} %constant.55.clone.inverse) | copy-start | bytes 786436
  46.4 0.9 %copy-start.1 = (bf16[512,256]{1,0:T(8,128)(2,1)S(1)}, bf16[512,256]{1,0:T(8,128)(2,1)}, u32[]{:S(2)}) copy-start(bf16[512,256]{1,0:T(8,128)(2,1)} %constant.54.clone.forward) | copy-start | bytes 786436
  47.4 0.7 copy-start.4
